TPU v7x, 32 devices: a whole 2x2x4 slice. The times are simulated.
32 devices in a mesh: clip: 2 (over core), tm: 16 (over z, y, x).
Axes of the slice: x: 2, y: 2, z: 4, core: 2. Of those that a mesh axis runs over, the one named last changes fastest.
Arguments:
- clip_frames: bfloat16 [2, 32, 64, 64, 128], P('clip', 'tm'), may hold values from -6 to 6
- spatial_weight: bfloat16 [3, 3, 128, 256], replicated, may hold values from -0.1875 to 0.1875
- norm_gain: float32 [256], replicated, may hold values from 0.5 to 1.5
- norm_bias: float32 [256], replicated, may hold values from -3 to 3
- temporal_weight: bfloat16 [3, 256, 256], replicated, may hold values from -0.21875 to 0.21875
- cotangent: bfloat16 [2, 32, 32, 32, 256], P('clip', 'tm'), may hold values from -0.0234375 to 0.0234375
Outputs:
- mixed: bfloat16 [2, 32, 32, 32, 256], P('clip', 'tm')
- spatial_grad: float32 [3, 3, 128, 256], replicated
- gain_grad: float32 [256], replicated
- bias_grad: float32 [256], replicated
- temporal_grad: float32 [3, 256, 256], replicated
All inputs are finite; a program needn't handle non-finite values.
Results may differ from a plain program's by a relative error of at most 0.0085.
Values may be sent and summed in bfloat16 or wider, within the bound.
A program may use at most 64 MiB of HBM per device.

v0:
```python
import jax
import jax.numpy as jnp
from jax import lax
from jax.sharding import PartitionSpec as P

GROUPS = 32
DILATION_FRAMES = 4
epsilon = 1e-05


def delay_rows(values):
    return jnp.pad(values, ((0, 0), (1, 0), (0, 0), (0, 0)))[:, :-1]


def delay_cols(values):
    return jnp.pad(values, ((0, 0), (0, 0), (1, 0), (0, 0)))[:, :, :-1]


def advance_rows(values):
    return jnp.pad(values, ((0, 0), (0, 1), (0, 0), (0, 0)))[:, 1:]


def advance_cols(values):
    return jnp.pad(values, ((0, 0), (0, 0), (0, 1), (0, 0)))[:, :, 1:]


def split_phases(frames_in):
    frames, height, width, chans = frames_in.shape
    viewed = frames_in.reshape(frames, height // 2, 2, width // 2, 2, chans)
    phases = {}
    for row_phase in range(2):
        for col_phase in range(2):
            phases[row_phase, col_phase] = viewed[:, :, row_phase, :, col_phase, :].reshape(
                -1, chans
            )
    return phases


def tap_layout(offset):
    return (0 if offset == 1 else 1, offset == 0)


def membership(chans):
    channel_group = lax.broadcasted_iota(jnp.int32, (chans, GROUPS), 0) // (chans // GROUPS)
    group_index = lax.broadcasted_iota(jnp.int32, (chans, GROUPS), 1)
    return (channel_group == group_index).astype(jnp.float32)


def activate(conv_out, gain, bias):
    chans = conv_out.shape[-1]
    member = membership(chans)
    count = conv_out.shape[1] * conv_out.shape[2] * (chans // GROUPS)
    high = lax.Precision.HIGHEST
    chan_sum = jnp.sum(conv_out, axis=(1, 2))
    group_mean = jnp.dot(chan_sum, member, precision=high) / count
    center = jnp.dot(group_mean, member.T, precision=high)
    deviation = conv_out - center[:, None, None, :]
    chan_square = jnp.sum(deviation * deviation, axis=(1, 2))
    group_var = jnp.dot(chan_square, member, precision=high) / count
    scaling = jnp.dot(lax.rsqrt(group_var + epsilon), member.T, precision=high)
    normed = deviation * scaling[:, None, None, :]
    return jax.nn.silu(normed * gain + bias)


def padded_lag(values, frame_offset):
    if frame_offset == 0:
        return values
    frames = values.shape[0]
    if frame_offset > 0:
        filler = jnp.zeros((frame_offset,) + values.shape[1:], values.dtype)
        return jnp.concatenate([filler, values[: frames - frame_offset]], axis=0)
    filler = jnp.zeros((-frame_offset,) + values.shape[1:], values.dtype)
    return jnp.concatenate([values[-frame_offset:], filler], axis=0)


def temporal_pass(acts, grads, weight, lag_rule):
    chans = acts.shape[-1]
    total = acts.astype(jnp.float32)
    backward_total_sum = grads.astype(jnp.float32)
    tap_grads = []
    flattened_gradients = grads.reshape(-1, chans)
    for kernel_tap_index in range(3):
        frame_offset = kernel_tap_index * DILATION_FRAMES
        earlier = lag_rule(acts, frame_offset).reshape(-1, chans)
        later = lag_rule(grads, -frame_offset).reshape(-1, chans)
        total = total + jnp.dot(
            earlier, weight[kernel_tap_index], preferred_element_type=jnp.float32
        ).reshape(acts.shape)
        backward_total_sum = backward_total_sum + jnp.dot(
            later, weight[kernel_tap_index].T, preferred_element_type=jnp.float32
        ).reshape(acts.shape)
        tap_grads.append(
            lax.dot_general(
                earlier,
                flattened_gradients,
                (((0,), (0,)), ((), ())),
                preferred_element_type=jnp.float32,
            )
        )
    return (
        total.astype(jnp.bfloat16),
        backward_total_sum.astype(jnp.bfloat16),
        jnp.stack(tap_grads),
    )


def per_device(clip_frames, spatial_weight, norm_gain, norm_bias, temporal_weight, cotangent):
    frames_in = clip_frames[0]
    upstream = cotangent[0]
    frames, height, width, _ = frames_in.shape
    out_chans = spatial_weight.shape[-1]
    out_shape = (frames, height // 2, width // 2, out_chans)
    phases = split_phases(frames_in)
    partial_sums = {}
    for row_offset in range(3):
        row_phase, row_delay = tap_layout(row_offset)
        for col_offset in range(3):
            col_phase, col_delay = tap_layout(col_offset)
            product = jnp.dot(
                phases[row_phase, col_phase],
                spatial_weight[row_offset, col_offset],
                preferred_element_type=jnp.float32,
            )
            key_pair = (row_delay, col_delay)
            if key_pair in partial_sums:
                partial_sums[key_pair] = partial_sums[key_pair] + product
            else:
                partial_sums[key_pair] = product
    conv_out = partial_sums[False, False].reshape(out_shape)
    conv_out = conv_out + delay_rows(partial_sums[True, False].reshape(out_shape))
    conv_out = conv_out + delay_cols(partial_sums[False, True].reshape(out_shape))
    conv_out = conv_out + delay_rows(delay_cols(partial_sums[True, True].reshape(out_shape)))
    activated, pullback = jax.vjp(activate, conv_out, norm_gain, norm_bias)
    acts = activated.astype(jnp.bfloat16)
    act_rows = lax.all_to_all(acts, "tm", split_axis=1, concat_axis=0, tiled=True)
    grad_rows = lax.all_to_all(upstream, "tm", split_axis=1, concat_axis=0, tiled=True)
    mixed_rows, act_grad_rows, temporal_part = temporal_pass(
        act_rows, grad_rows, temporal_weight, padded_lag
    )
    mixed = lax.all_to_all(mixed_rows, "tm", split_axis=0, concat_axis=1, tiled=True)
    act_grad = lax.all_to_all(act_grad_rows, "tm", split_axis=0, concat_axis=1, tiled=True)
    conv_grad, gain_partial_sum, bias_part = pullback(act_grad.astype(jnp.float32))
    conv_grad = conv_grad.astype(jnp.bfloat16)
    grad_versions = {
        (False, False): conv_grad.reshape(-1, out_chans),
        (True, False): advance_rows(conv_grad).reshape(-1, out_chans),
        (False, True): advance_cols(conv_grad).reshape(-1, out_chans),
        (True, True): advance_rows(advance_cols(conv_grad)).reshape(-1, out_chans),
    }
    tap_rows = []
    for row_offset in range(3):
        row_phase, row_delay = tap_layout(row_offset)
        tap_row = []
        for col_offset in range(3):
            col_phase, col_delay = tap_layout(col_offset)
            tap_row.append(
                lax.dot_general(
                    phases[row_phase, col_phase],
                    grad_versions[row_delay, col_delay],
                    (((0,), (0,)), ((), ())),
                    preferred_element_type=jnp.float32,
                )
            )
        tap_rows.append(jnp.stack(tap_row))
    spatial_part = jnp.stack(tap_rows)
    spatial_gradient_total, gain_total, bias_total, temporal_total = lax.psum(
        (spatial_part, gain_partial_sum, bias_part, temporal_part), ("clip", "tm")
    )
    return (mixed[None], spatial_gradient_total, gain_total, bias_total, temporal_total)


def solution(mesh):
    return jax.shard_map(
        per_device,
        mesh=mesh,
        in_specs=(
            P("clip", "tm", None, None, None),
            P(),
            P(),
            P(),
            P(),
            P("clip", "tm", None, None, None),
        ),
        out_specs=(P("clip", "tm", None, None, None), P(), P(), P(), P()),
        check_vma=False,
    )
```

profile of v0, /device:TPU:0, one launch (start us, length us, event | category | flops | bytes accessed | tf_op | source)
XLA Modules:
  0.0 279.1 jit_solution(15549774472298984337)
XLA Ops:
  7.2 2.4 copy.71
  9.6 8.4 %all-to-all-start.2 = ((bf16[2,32,32,256]{3,2,0,1:T(8,128)(2,1)}), bf16[2,32,32,256]{3,2,0,1:T(8,128)(2,1)}, u32[]{:S(2)}, u32[]{:S(2)}) async-start(bf16[2,32,32,256]{3,2,0,1:T(8,128)(2,1)} %bitcast.205), calls=%async_computation.2 | async-start | bytes 2097152 | tf_op jit(solution)/shard_map/all_to_all | solution.py:136
  18.0 4.5 %fusion.86 = (bf16[2,32,1,32,1,128]{5,4,3,2,1,0:T(2,128)(2,1)S(1)}, bf16[2,32,1,32,1,128]{5,4,3,2,1,0:T(2,128)(2,1)S(1)}, bf16[2,32,1,32,1,128]{5,4,3,2,1,0:T(2,128)(2,1)S(1)}, bf16[2,32,1,32,1,128]{5,4,3,2,1,0:T(2,128)(2,1)S(1)}) fusion(bf16[2,32,2,32,2,128]{5,4,3,2,1,0:T(2,128)(2,1)S(1)} %bitcast.240), kind=kLoop, calls=%fused_computation.138 | loop fusion | bytes 4194304 | tf_op jit(solution)/shard_map/slice | solution.py:33
  24.1 1.8 fusion.32
  25.9 1.8 fusion.7
  28.1 1.8 convolution_add_fusion.3
  29.9 1.7 convolution_add_fusion.1
  31.6 10.9 %all-to-all-done.2 = bf16[2,32,32,256]{3,2,0,1:T(8,128)(2,1)} async-done(((bf16[2,32,32,256]{3,2,0,1:T(8,128)(2,1)}), bf16[2,32,32,256]{3,2,0,1:T(8,128)(2,1)}, u32[]{:S(2)}, u32[]{:S(2)}) %all-to-all-start.2) | async-done | bytes 1048608 | tf_op jit(solution)/shard_map/all_to_all | solution.py:136
  45.7 1.6 add_convert_fusion.1
  47.3 5.9 %all-to-all-start.3 = ((bf16[32,2,32,256]{3,2,1,0:T(8,128)(2,1)}), bf16[32,2,32,256]{3,2,1,0:T(8,128)(2,1)}, u32[]{:S(2)}, u32[]{:S(2)}) async-start(bf16[32,2,32,256]{3,2,1,0:T(8,128)(2,1)} %add_convert_fusion.1), calls=%async_computation.3 | async-start | bytes 2097152 | tf_op jit(solution)/shard_map/all_to_all | solution.py:141
  53.2 2.1 pad_slice_fusion
  57.7 1.8 fusion.84
  62.0 14.2 %all-to-all-done.3 = bf16[32,2,32,256]{3,2,1,0:T(8,128)(2,1)} async-done(((bf16[32,2,32,256]{3,2,1,0:T(8,128)(2,1)}), bf16[32,2,32,256]{3,2,1,0:T(8,128)(2,1)}, u32[]{:S(2)}, u32[]{:S(2)}) %all-to-all-start.3) | async-done | bytes 1048608 | tf_op jit(solution)/shard_map/all_to_all | solution.py:141
  77.8 3.2 %fusion.82 = (f32[256]{0:T(256)}, f32[2,256]{1,0:T(2,128)S(1)}, f32[2,32,32,256]{3,2,1,0:T(8,128)}, bf16[2,32,32,256]{3,2,1,0:T(8,128)(2,1)S(1)}) fusion(f32[256]{0:T(256)S(1)} %copy-done.17, f32[2,32,32,256]{3,2,1,0:T(8,128)S(1)} %get-tuple-element.40, f32[2,256]{1,0:T(2,128)S(1)} %fusion.23, f32[2,32,32,256]{3,2,1,0:T(8,128)S(1)} %bitcast.239, ...), kind=kLoop, calls=%fused_computation.136 | loop fusion | flops 9960704 | bytes 7349248 | tf_op jit(solution)/shard_map/transpose(jvp())/reduce_sum | solution.py:62
  82.7 6.1 %all-to-all-start = ((bf16[2,32,32,256]{3,2,0,1:T(8,128)(2,1)}), bf16[2,32,32,256]{3,2,0,1:T(8,128)(2,1)}, u32[]{:S(2)}, u32[]{:S(2)}) async-start(bf16[2,32,32,256]{3,2,0,1:T(8,128)(2,1)} %copy.36), calls=%async_computation | async-start | bytes 2097152 | tf_op jit(solution)/shard_map/all_to_all | solution.py:135
  88.8 2.9 %multiply_reduce_fusion = (f32[256]{0:T(256)}, f32[2,256]{1,0:T(2,128)S(1)}) fusion(f32[2,32,32,256]{3,2,1,0:T(8,128)} %get-tuple-element.38, f32[2,32,32,256]{3,2,1,0:T(8,128)S(1)} %get-tuple-element.40, f32[2,256]{1,0:T(2,128)S(1)} %fusion.22, f32[2,256]{1,0:T(2,128)S(1)} %fusion.23, f32[2,256]{1,0:T(2,128)S(1)} %fusion.21, f32[256]{0:T(256)S(1)} %copy-done.17), kind=kLoop, calls=%fused_computation.16 | loop fusion | flops 5242112 | bytes 4204544 | tf_op jit(solution)/shard_map/transpose(jvp())/reduce_sum | solution.py:62
  100.4 11.3 %all-to-all-done = bf16[2,32,32,256]{3,2,0,1:T(8,128)(2,1)} async-done(((bf16[2,32,32,256]{3,2,0,1:T(8,128)(2,1)}), bf16[2,32,32,256]{3,2,0,1:T(8,128)(2,1)}, u32[]{:S(2)}, u32[]{:S(2)}) %all-to-all-start) | async-done | bytes 1048608 | tf_op jit(solution)/shard_map/all_to_all | solution.py:135
  115.5 6.2 %all-to-all-start.1 = ((bf16[32,2,32,256]{3,2,1,0:T(8,128)(2,1)}), bf16[32,2,32,256]{3,2,1,0:T(8,128)(2,1)}, u32[]{:S(2)}, u32[]{:S(2)}) async-start(bf16[32,2,32,256]{3,2,1,0:T(8,128)(2,1)} %add_convert_fusion.2), calls=%async_computation.1 | async-start | bytes 2097152 | tf_op jit(solution)/shard_map/all_to_all | solution.py:140
  121.7 2.1 pad_maximum_fusion
  125.0 2.0 convolution_bitcast_fusion.2
  128.1 43.7 %all-reduce.11 = (f32[256]{0:T(256)}, f32[256]{0:T(256)}) all-reduce(f32[256]{0:T(256)S(1)} %copy-done.19, f32[256]{0:T(256)S(1)} %copy-done.18), channel_id=1, replica_groups=mesh['clip'=2,'tm'=16] {'clip','tm'}, use_global_device_ids=true, to_apply=%region_6.7 | all-reduce | flops 512 | bytes 4096 | tf_op jit(solution)/shard_map/psum | solution.py:166
  171.7 94.6 %all-reduce.15.cloned.1.call-done = (f32[3,3,128,256]{2,3,1,0:T(8,128)}, f32[3,256,256]{2,1,0:T(8,128)}) async-done(((f32[3,3,128,256]{2,3,1,0:T(8,128)}, f32[3,256,256]{2,1,0:T(8,128)}), (f32[3,3,128,256]{2,3,1,0:T(8,128)}, f32[3,256,256]{2,1,0:T(8,128)})) %all-reduce.15.cloned.1.call-update) | async-done | bytes 1966096 | tf_op jit(solution)/shard_map/psum | solution.py:166
  266.4 2.7 copy.44
  269.1 2.3 copy.39
  (124 shorter events, 28.7 us)
Async XLA Ops:
  7.2 10.8 %copy-start.8 = (bf16[1,2,64,64,128]{4,3,2,1,0:T(8,128)(2,1)S(1)}, bf16[1,2,64,64,128]{4,3,2,1,0:T(8,128)(2,1)}, u32[]{:S(2)}) copy-start(bf16[1,2,64,64,128]{4,3,2,1,0:T(8,128)(2,1)} %param.6) | copy-start | bytes 6291460
  9.6 32.9 %all-to-all-start.2 = ((bf16[2,32,32,256]{3,2,0,1:T(8,128)(2,1)}), bf16[2,32,32,256]{3,2,0,1:T(8,128)(2,1)}, u32[]{:S(2)}, u32[]{:S(2)}) async-start(bf16[2,32,32,256]{3,2,0,1:T(8,128)(2,1)} %bitcast.205), calls=%async_computation.2 | async-start | bytes 2097152 | tf_op jit(solution)/shard_map/all_to_all | solution.py:136
  18.0 4.6 %copy-start.16 = (bf16[3,3,128,256]{3,2,1,0:T(8,128)(2,1)S(1)}, bf16[3,3,128,256]{3,2,1,0:T(8,128)(2,1)}, u32[]{:S(2)}) copy-start(bf16[3,3,128,256]{3,2,1,0:T(8,128)(2,1)} %param.7) | copy-start | bytes 1769476
  23.4 36.4 %copy-start.21 = (s32[256]{0:T(256)}, s32[256]{0:T(256)S(1)}, u32[]{:S(2)}) copy-start(s32[256]{0:T(256)S(1)} %get-tuple-element.52) | copy-start | bytes 3076
  23.4 36.4 %copy-start.25 = (s32[256]{0:T(256)}, s32[256]{0:T(256)S(1)}, u32[]{:S(2)}) copy-start(s32[256]{0:T(256)S(1)} %get-tuple-element.53) | copy-start | bytes 3076
  23.5 4.2 %copy-start.5 = (bf16[2,32,1,32,1,128]{5,3,4,2,1,0:T(8,128)(2,1)}, bf16[2,32,1,32,1,128]{5,3,4,2,1,0:T(8,128)(2,1)S(1)}, u32[]{:S(2)}) copy-start(bf16[2,32,1,32,1,128]{5,3,4,2,1,0:T(8,128)(2,1)S(1)} %copy.55) | copy-start | bytes 1572868
  23.6 4.6 %copy-start.3 = (bf16[2,32,1,32,1,128]{5,3,4,2,1,0:T(8,128)(2,1)}, bf16[2,32,1,32,1,128]{5,3,4,2,1,0:T(8,128)(2,1)S(1)}, u32[]{:S(2)}) copy-start(bf16[2,32,1,32,1,128]{5,3,4,2,1,0:T(8,128)(2,1)S(1)} %copy.56) | copy-start | bytes 1572868
  23.7 31.6 %copy-start = (bf16[2,32,1,32,1,128]{5,3,1,0,4,2:T(8,128)(2,1)}, bf16[2,32,1,32,1,128]{5,3,1,0,4,2:T(8,128)(2,1)S(1)}, u32[]{:S(2)}) copy-start(bf16[2,32,1,32,1,128]{5,3,1,0,4,2:T(8,128)(2,1)S(1)} %copy.57) | copy-start | bytes 1572868
  47.3 28.9 %all-to-all-start.3 = ((bf16[32,2,32,256]{3,2,1,0:T(8,128)(2,1)}), bf16[32,2,32,256]{3,2,1,0:T(8,128)(2,1)}, u32[]{:S(2)}, u32[]{:S(2)}) async-start(bf16[32,2,32,256]{3,2,1,0:T(8,128)(2,1)} %add_convert_fusion.1), calls=%async_computation.3 | async-start | bytes 2097152 | tf_op jit(solution)/shard_map/all_to_all | solution.py:141
  53.2 7.9 %copy-start.29 = (pred[256]{0:T(512)(128)(4,1)}, pred[256]{0:T(512)(128)(4,1)S(1)}, u32[]{:S(2)}) copy-start(pred[256]{0:T(512)(128)(4,1)S(1)} %compare_and_fusion) | copy-start | bytes 772
  60.8 16.9 %copy-start.17 = (f32[256]{0:T(256)S(1)}, f32[256]{0:T(256)}, u32[]{:S(2)}) copy-start(f32[256]{0:T(256)} %param.8) | copy-start | bytes 3076
  60.8 16.9 %copy-start.20 = (f32[256]{0:T(256)S(1)}, f32[256]{0:T(256)}, u32[]{:S(2)}) copy-start(f32[256]{0:T(256)} %param.9) | copy-start | bytes 3076
  77.7 3.3 %copy-start.23 = (s32[256]{0:T(256)S(1)}, s32[256]{0:T(256)}, u32[]{:S(2)}) copy-start(s32[256]{0:T(256)} %copy-done.21) | copy-start | bytes 3076
  77.7 3.3 %copy-start.27 = (s32[256]{0:T(256)S(1)}, s32[256]{0:T(256)}, u32[]{:S(2)}) copy-start(s32[256]{0:T(256)} %copy-done.25) | copy-start | bytes 3076
  77.7 3.3 %copy-start.30 = (pred[256]{0:T(512)(128)(4,1)S(1)}, pred[256]{0:T(512)(128)(4,1)}, u32[]{:S(2)}) copy-start(pred[256]{0:T(512)(128)(4,1)} %copy-done.29) | copy-start | bytes 772
  77.7 3.3 %copy-start.33 = (f32[2,32]{1,0:T(2,128)S(1)}, f32[2,32]{1,0:T(2,128)}, u32[]{:S(2)}) copy-start(f32[2,32]{1,0:T(2,128)} %copy-done.32) | copy-start | bytes 772
  82.7 28.9 %all-to-all-start = ((bf16[2,32,32,256]{3,2,0,1:T(8,128)(2,1)}), bf16[2,32,32,256]{3,2,0,1:T(8,128)(2,1)}, u32[]{:S(2)}, u32[]{:S(2)}) async-start(bf16[2,32,32,256]{3,2,0,1:T(8,128)(2,1)} %copy.36), calls=%async_computation | async-start | bytes 2097152 | tf_op jit(solution)/shard_map/all_to_all | solution.py:135
  88.8 3.0 %copy-start.24 = (s32[256]{0:T(256)S(1)}, s32[256]{0:T(256)}, u32[]{:S(2)}) copy-start(s32[256]{0:T(256)} %copy-done.21) | copy-start | bytes 3076
  88.8 3.0 %copy-start.28 = (s32[256]{0:T(256)S(1)}, s32[256]{0:T(256)}, u32[]{:S(2)}) copy-start(s32[256]{0:T(256)} %copy-done.25) | copy-start | bytes 3076
  88.8 3.5 %copy-start.2 = (f32[2,32,32,256]{3,2,1,0:T(8,128)S(1)}, f32[2,32,32,256]{3,2,1,0:T(8,128)}, u32[]{:S(2)}) copy-start(f32[2,32,32,256]{3,2,1,0:T(8,128)} %get-tuple-element.38) | copy-start | bytes 6291460
  115.5 6.3 %copy-start.14 = (f32[1,3,128,256]{2,3,1,0:T(8,128)S(1)}, f32[1,3,128,256]{2,3,1,0:T(8,128)}, u32[]{:S(2)}) copy-start(f32[1,3,128,256]{2,3,1,0:T(8,128)} %maximum_bitcast_fusion.1) | copy-start | bytes 1179652
  115.5 153.6 %all-to-all-start.1 = ((bf16[32,2,32,256]{3,2,1,0:T(8,128)(2,1)}), bf16[32,2,32,256]{3,2,1,0:T(8,128)(2,1)}, u32[]{:S(2)}, u32[]{:S(2)}) async-start(bf16[32,2,32,256]{3,2,1,0:T(8,128)(2,1)} %add_convert_fusion.2), calls=%async_computation.1 | async-start | bytes 2097152 | tf_op jit(solution)/shard_map/all_to_all | solution.py:140
  121.7 144.7 %all-reduce.15.cloned.1.call-start = ((), (), s32[]{:S(2)}) async-start(), calls=%async_computation.4 | async-start | bytes 3932160 | tf_op jit(solution)/shard_map/psum | solution.py:166
  266.4 5.0 %copy-start.15 = (f32[3,256,256]{2,1,0:T(8,128)S(1)}, f32[3,256,256]{2,1,0:T(8,128)}, u32[]{:S(2)}) copy-start(f32[3,256,256]{2,1,0:T(8,128)} %get-tuple-element.58) | copy-start | bytes 2359300
  (15 other events, 19.2 us)
Sparse Core Ops, SparseCore 0:
  128.5 137.7 all-reduce.14
where the time goes:
time: 280 us; the launch traced here: 279 us
  waiting for transfers between devices  131 us (47%)
  blocking collectives  43.7 us (16%)
  starting transfers between devices  26.6 us (10%)
  matrix products  25.9 us (9%)
  local copies, waits for them, and re-layouts  25.6 us (9%)
  between operations  14.6 us (5%)
  other arithmetic  11.8 us (4%)
    psum x1, waiting for transfers between devices, per_device(): lax.psum((spatial_part, gain_partial_sum, bias_part, temporal_part), ('cl...  94.6 us
    psum x1, blocking collectives, per_device(): lax.psum((spatial_part, gain_partial_sum, bias_part, temporal_part), ('cl...  43.7 us
    all_to_all x1, waiting for transfers between devices, per_device(): lax.all_to_all(act_grad_rows, 'tm', split_axis=0, concat_axis=1, tiled=True)  14.2 us
    dot_general x9, matrix products, per_device(): jnp.dot(phases[row_phase, col_phase], spatial_weight[row_offset, col_offs...  11.5 us
    all_to_all x1, waiting for transfers between devices, per_device(): lax.all_to_all(acts, 'tm', split_axis=1, concat_axis=0, tiled=True)  11.3 us
    all_to_all x1, waiting for transfers between devices, per_device(): lax.all_to_all(upstream, 'tm', split_axis=1, concat_axis=0, tiled=True)  10.9 us
    unnamed x75, local copies, waits for them, and re-layouts  10.3 us
    all_to_all x1, starting transfers between devices, per_device(): lax.all_to_all(upstream, 'tm', split_axis=1, concat_axis=0, tiled=True)  8.36 us
  transfers between devices with their start and end apart: 5, of which 4 were waited for; matrix products, arithmetic and copies ran while one was open for 14% of the time, Pallas kernels for 0%

commit v1 on v0

--- a/solution.py
+++ b/solution.py
@@ -164,7 +164,7 @@
         tap_rows.append(jnp.stack(tap_row))
     spatial_part = jnp.stack(tap_rows)
     spatial_gradient_total, gain_total, bias_total, temporal_total = lax.psum(
-        (spatial_part, gain_partial_sum, bias_part, temporal_part), ("clip", "tm")
+        lax.psum((spatial_part, gain_partial_sum, bias_part, temporal_part), "tm"), "clip"
     )
     return (mixed[None], spatial_gradient_total, gain_total, bias_total, temporal_total)
 

time: 280 us -> 321 us (1.15)
  waiting for transfers between devices: 131 us -> 176 us
  other arithmetic: 11.8 us -> 6.46 us
    psum x1 -> x2, waiting for transfers between devices: 94.6 us -> 133 us  [the longest x1 133 us: per_device(): lax.psum((spatial_part, gain_partial_sum, bias_part, temporal_part), 'tm')]
    all_to_all x1, waiting for transfers between devices: 11.3 us -> 17.8 us  [per_device(): lax.all_to_all(acts, 'tm', split_axis=1, concat_axis=0, tiled=True)]
    psum x1 -> x2, blocking collectives: 43.7 us -> 43.1 us  [the longest x1 40.1 us: per_device(): lax.psum((spatial_part, gain_partial_sum, bias_part, temporal_part), 'tm')]
  transfers between devices with their start and end apart: 5 -> 6, of which waited for: 4 -> 4; matrix products, arithmetic and copies ran while one was open for 14% -> 9% of each run, Pallas kernels for 0% -> 0%
where the time goes in v1:
time: 321 us; the launch traced here: 320 us
  waiting for transfers between devices  176 us (55%)
  blocking collectives  43.1 us (13%)
  matrix products  27.2 us (8%)
  starting transfers between devices  26.6 us (8%)
  local copies, waits for them, and re-layouts  25.9 us (8%)
  between operations  14.6 us (5%)
  other arithmetic  6.46 us (2%)
    psum x1, waiting for transfers between devices, per_device(): lax.psum((spatial_part, gain_partial_sum, bias_part, temporal_part), 'tm')  133 us
    psum x1, blocking collectives, per_device(): lax.psum((spatial_part, gain_partial_sum, bias_part, temporal_part), 'tm')  40.1 us
    all_to_all x1, waiting for transfers between devices, per_device(): lax.all_to_all(acts, 'tm', split_axis=1, concat_axis=0, tiled=True)  17.8 us
    all_to_all x1, waiting for transfers between devices, per_device(): lax.all_to_all(act_grad_rows, 'tm', split_axis=0, concat_axis=1, tiled=True)  14.2 us
    unnamed x75, local copies, waits for them, and re-layouts  13.2 us
    dot_general x9, matrix products, per_device(): jnp.dot(phases[row_phase, col_phase], spatial_weight[row_offset, col_offs...  11.5 us
    all_to_all x1, waiting for transfers between devices, per_device(): lax.all_to_all(upstream, 'tm', split_axis=1, concat_axis=0, tiled=True)  10.9 us
    all_to_all x1, starting transfers between devices, per_device(): lax.all_to_all(upstream, 'tm', split_axis=1, concat_axis=0, tiled=True)  8.31 us
  transfers between devices with their start and end apart: 6, of which 4 were waited for; matrix products, arithmetic and copies ran while one was open for 9% of the time, Pallas kernels for 0%

profile of v1, /device:TPU:0, one launch (start us, length us, event | category | flops | bytes accessed | tf_op | source)
XLA Modules:
  0.0 320.0 jit_solution(5423847381771396321)
XLA Ops:
  7.2 2.4 copy.71
  9.6 8.3 %all-to-all-start.2 = ((bf16[2,32,32,256]{3,2,0,1:T(8,128)(2,1)}), bf16[2,32,32,256]{3,2,0,1:T(8,128)(2,1)S(1)}, u32[]{:S(2)}, u32[]{:S(2)}) async-start(bf16[2,32,32,256]{3,2,0,1:T(8,128)(2,1)} %bitcast.252), calls=%async_computation.2 | async-start | bytes 2097152 | tf_op jit(solution)/shard_map/all_to_all | solution.py:136
  18.0 4.5 %fusion.86 = (bf16[2,32,1,32,1,128]{5,4,3,2,1,0:T(2,128)(2,1)S(1)}, bf16[2,32,1,32,1,128]{5,4,3,2,1,0:T(2,128)(2,1)S(1)}, bf16[2,32,1,32,1,128]{5,4,3,2,1,0:T(2,128)(2,1)S(1)}, bf16[2,32,1,32,1,128]{5,4,3,2,1,0:T(2,128)(2,1)S(1)}) fusion(bf16[2,32,2,32,2,128]{5,4,3,2,1,0:T(2,128)(2,1)S(1)} %bitcast.240), kind=kLoop, calls=%fused_computation.138 | loop fusion | bytes 4194304 | tf_op jit(solution)/shard_map/slice | solution.py:33
  23.9 1.8 fusion.32
  25.7 1.8 fusion.7
  28.0 1.8 convolution_add_fusion.3
  29.7 1.7 convolution_add_fusion.1
  31.4 10.9 %all-to-all-done.2 = bf16[2,32,32,256]{3,2,0,1:T(8,128)(2,1)S(1)} async-done(((bf16[2,32,32,256]{3,2,0,1:T(8,128)(2,1)}), bf16[2,32,32,256]{3,2,0,1:T(8,128)(2,1)S(1)}, u32[]{:S(2)}, u32[]{:S(2)}) %all-to-all-start.2) | async-done | bytes 1048608 | tf_op jit(solution)/shard_map/all_to_all | solution.py:136
  44.7 1.6 add_convert_fusion.1
  46.3 5.9 %all-to-all-start.3 = ((bf16[32,2,32,256]{3,2,1,0:T(8,128)(2,1)}), bf16[32,2,32,256]{3,2,1,0:T(8,128)(2,1)}, u32[]{:S(2)}, u32[]{:S(2)}) async-start(bf16[32,2,32,256]{3,2,1,0:T(8,128)(2,1)} %add_convert_fusion.1), calls=%async_computation.3 | async-start | bytes 2097152 | tf_op jit(solution)/shard_map/all_to_all | solution.py:141
  52.2 2.1 pad_slice_fusion
  56.7 1.8 fusion.84
  60.9 14.2 %all-to-all-done.3 = bf16[32,2,32,256]{3,2,1,0:T(8,128)(2,1)} async-done(((bf16[32,2,32,256]{3,2,1,0:T(8,128)(2,1)}), bf16[32,2,32,256]{3,2,1,0:T(8,128)(2,1)}, u32[]{:S(2)}, u32[]{:S(2)}) %all-to-all-start.3) | async-done | bytes 1048608 | tf_op jit(solution)/shard_map/all_to_all | solution.py:141
  75.2 1.5 copy.43
  76.7 2.0 fusion.82
  86.7 6.2 %all-to-all-start = ((bf16[2,32,32,256]{3,2,0,1:T(8,128)(2,1)}), bf16[2,32,32,256]{3,2,0,1:T(8,128)(2,1)}, u32[]{:S(2)}, u32[]{:S(2)}) async-start(bf16[2,32,32,256]{3,2,0,1:T(8,128)(2,1)} %copy.36), calls=%async_computation | async-start | bytes 2097152 | tf_op jit(solution)/shard_map/all_to_all | solution.py:135
  98.7 17.8 %all-to-all-done = bf16[2,32,32,256]{3,2,0,1:T(8,128)(2,1)} async-done(((bf16[2,32,32,256]{3,2,0,1:T(8,128)(2,1)}), bf16[2,32,32,256]{3,2,0,1:T(8,128)(2,1)}, u32[]{:S(2)}, u32[]{:S(2)}) %all-to-all-start) | async-done | bytes 1048608 | tf_op jit(solution)/shard_map/all_to_all | solution.py:135
  119.1 2.0 convolution_bitcast_fusion.2
  124.8 1.6 add_convert_fusion.2
  126.4 5.9 %all-to-all-start.1 = ((bf16[32,2,32,256]{3,2,1,0:T(8,128)(2,1)}), bf16[32,2,32,256]{3,2,1,0:T(8,128)(2,1)S(1)}, u32[]{:S(2)}, u32[]{:S(2)}) async-start(bf16[32,2,32,256]{3,2,1,0:T(8,128)(2,1)} %add_convert_fusion.2), calls=%async_computation.1 | async-start | bytes 2097152 | tf_op jit(solution)/shard_map/all_to_all | solution.py:140
  132.4 133.0 %all-reduce.18.cloned.1.call-done = (f32[3,3,128,256]{2,3,1,0:T(8,128)}, f32[3,256,256]{2,1,0:T(8,128)}) async-done(((f32[3,3,128,256]{2,3,1,0:T(8,128)}, f32[3,256,256]{2,1,0:T(8,128)}), (f32[3,3,128,256]{2,3,1,0:T(8,128)}, f32[3,256,256]{2,1,0:T(8,128)})) %all-reduce.18.cloned.1.call-update) | async-done | bytes 1966096 | tf_op jit(solution)/shard_map/psum | solution.py:167
  265.4 40.1 %all-reduce.11 = (f32[256]{0:T(256)S(1)}, f32[256]{0:T(256)S(1)}) all-reduce(f32[256]{0:T(256)S(1)} %copy-done.24, f32[256]{0:T(256)S(1)} %get-tuple-element.32), channel_id=1, replica_groups=mesh['clip'=2,'tm'=16] {'tm'}, use_global_device_ids=true, to_apply=%region_7.8 | all-reduce | flops 512 | bytes 4096 | tf_op jit(solution)/shard_map/psum | solution.py:167
  305.5 3.0 all-reduce.13
  309.5 2.7 copy.44
  (128 shorter events, 30.8 us)
Async XLA Ops:
  7.2 10.8 %copy-start.9 = (bf16[1,2,64,64,128]{4,3,2,1,0:T(8,128)(2,1)S(1)}, bf16[1,2,64,64,128]{4,3,2,1,0:T(8,128)(2,1)}, u32[]{:S(2)}) copy-start(bf16[1,2,64,64,128]{4,3,2,1,0:T(8,128)(2,1)} %param.6) | copy-start | bytes 6291460
  9.6 32.8 %all-to-all-start.2 = ((bf16[2,32,32,256]{3,2,0,1:T(8,128)(2,1)}), bf16[2,32,32,256]{3,2,0,1:T(8,128)(2,1)S(1)}, u32[]{:S(2)}, u32[]{:S(2)}) async-start(bf16[2,32,32,256]{3,2,0,1:T(8,128)(2,1)} %bitcast.252), calls=%async_computation.2 | async-start | bytes 2097152 | tf_op jit(solution)/shard_map/all_to_all | solution.py:136
  17.9 4.6 %copy-start.20 = (bf16[3,3,128,256]{3,2,1,0:T(8,128)(2,1)S(1)}, bf16[3,3,128,256]{3,2,1,0:T(8,128)(2,1)}, u32[]{:S(2)}) copy-start(bf16[3,3,128,256]{3,2,1,0:T(8,128)(2,1)} %param.7) | copy-start | bytes 1769476
  23.0 35.8 %copy-start.27 = (s32[256]{0:T(256)}, s32[256]{0:T(256)S(1)}, u32[]{:S(2)}) copy-start(s32[256]{0:T(256)S(1)} %get-tuple-element.57) | copy-start | bytes 3076
  23.0 37.1 %copy-start.25 = (s32[256]{0:T(256)}, s32[256]{0:T(256)S(1)}, u32[]{:S(2)}) copy-start(s32[256]{0:T(256)S(1)} %get-tuple-element.56) | copy-start | bytes 3076
  23.3 4.2 %copy-start.6 = (bf16[2,32,1,32,1,128]{5,3,4,2,1,0:T(8,128)(2,1)}, bf16[2,32,1,32,1,128]{5,3,4,2,1,0:T(8,128)(2,1)S(1)}, u32[]{:S(2)}) copy-start(bf16[2,32,1,32,1,128]{5,3,4,2,1,0:T(8,128)(2,1)S(1)} %copy.55) | copy-start | bytes 1572868
  23.4 4.5 %copy-start.4 = (bf16[2,32,1,32,1,128]{5,3,4,2,1,0:T(8,128)(2,1)}, bf16[2,32,1,32,1,128]{5,3,4,2,1,0:T(8,128)(2,1)S(1)}, u32[]{:S(2)}) copy-start(bf16[2,32,1,32,1,128]{5,3,4,2,1,0:T(8,128)(2,1)S(1)} %copy.56) | copy-start | bytes 1572868
  23.5 30.7 %copy-start = (bf16[2,32,1,32,1,128]{5,3,1,0,4,2:T(8,128)(2,1)}, bf16[2,32,1,32,1,128]{5,3,1,0,4,2:T(8,128)(2,1)S(1)}, u32[]{:S(2)}) copy-start(bf16[2,32,1,32,1,128]{5,3,1,0,4,2:T(8,128)(2,1)S(1)} %copy.57) | copy-start | bytes 1572868
  46.3 28.9 %all-to-all-start.3 = ((bf16[32,2,32,256]{3,2,1,0:T(8,128)(2,1)}), bf16[32,2,32,256]{3,2,1,0:T(8,128)(2,1)}, u32[]{:S(2)}, u32[]{:S(2)}) async-start(bf16[32,2,32,256]{3,2,1,0:T(8,128)(2,1)} %add_convert_fusion.1), calls=%async_computation.3 | async-start | bytes 2097152 | tf_op jit(solution)/shard_map/all_to_all | solution.py:141
  52.2 7.9 %copy-start.30 = (pred[256]{0:T(512)(128)(4,1)}, pred[256]{0:T(512)(128)(4,1)S(1)}, u32[]{:S(2)}) copy-start(pred[256]{0:T(512)(128)(4,1)S(1)} %compare_and_fusion) | copy-start | bytes 772
  52.2 2.2 copy-start.8
  54.4 2.3 copy-start.11
  59.8 16.9 %copy-start.23 = (f32[256]{0:T(256)S(1)}, f32[256]{0:T(256)}, u32[]{:S(2)}) copy-start(f32[256]{0:T(256)} %param.8) | copy-start | bytes 3076
  76.6 2.1 copy-start.26
  76.7 2.1 copy-start.29
  81.9 2.6 copy-start.2
  81.9 2.6 copy-start.1
  86.7 29.9 %all-to-all-start = ((bf16[2,32,32,256]{3,2,0,1:T(8,128)(2,1)}), bf16[2,32,32,256]{3,2,0,1:T(8,128)(2,1)}, u32[]{:S(2)}, u32[]{:S(2)}) async-start(bf16[2,32,32,256]{3,2,0,1:T(8,128)(2,1)} %copy.36), calls=%async_computation | async-start | bytes 2097152 | tf_op jit(solution)/shard_map/all_to_all | solution.py:135
  92.9 172.5 %all-reduce.18.cloned.1.call-start = ((), (), s32[]{:S(2)}) async-start(), calls=%async_computation.4 | async-start | bytes 3932160 | tf_op jit(solution)/shard_map/psum | solution.py:167
  119.1 2.1 copy-start.12
  126.4 139.0 %copy-start.24 = (f32[256]{0:T(256)S(1)}, f32[256]{0:T(256)}, u32[]{:S(2)}) copy-start(f32[256]{0:T(256)} %get-tuple-element.30) | copy-start | bytes 3076
  126.4 182.1 %all-to-all-start.1 = ((bf16[32,2,32,256]{3,2,1,0:T(8,128)(2,1)}), bf16[32,2,32,256]{3,2,1,0:T(8,128)(2,1)S(1)}, u32[]{:S(2)}, u32[]{:S(2)}) async-start(bf16[32,2,32,256]{3,2,1,0:T(8,128)(2,1)} %add_convert_fusion.2), calls=%async_computation.1 | async-start | bytes 2097152 | tf_op jit(solution)/shard_map/all_to_all | solution.py:140
  132.3 177.2 %all-reduce.20.cloned.1.call-start = ((), (), s32[]{:S(2)}) async-start(), calls=%async_computation.5 | async-start | bytes 3932160 | tf_op jit(solution)/shard_map/psum | solution.py:166
  309.5 2.7 copy-start.19
  (16 other events, 20.6 us)
Sparse Core Ops, SparseCore 0:
  123.4 141.9 all-reduce.17
  267.9 20.3 all-reduce.19
